TPU v7x, 512 devices: a whole 4x4x16 slice. The times are simulated.
512 devices in a mesh: ifg: 128 (over x, z, core), tile: 4 (over y).
Axes of the slice: x: 4, y: 4, z: 16, core: 2. Of those that a mesh axis runs over, the one named last changes fastest.
Arguments:
- ifgs: bfloat16 [1152, 8, 16384], P('ifg', 'tile'), may hold values from -12 to 12
- pairs: int32 [1152, 2], replicated, may hold values from 0 to 299, as said below
- pseudo_inverse: bfloat16 [300, 1152], P(None, 'ifg'), may hold values from -0.1875 to 0.1875
- ref_pixels: int32 [64], replicated, may hold values from 0 to 131071
- epochs: int32 [8], replicated, may hold values from 8 to 291
Outputs:
- coefficients: float32 [16, 8, 16384], P(None, 'tile', 'ifg')
- misfit_rms: float32 [8, 16384], P('tile', 'ifg')
Inputs may be any that keep to these rules, and one draw needn't show every extreme that they name: pairs[k, 0] < pairs[k, 1] <= pairs[k, 0] + 6.
All inputs are finite; a program needn't handle non-finite values.
Results may differ from a plain program's by a relative error of at most 0.0029.
Values may be sent and summed in bfloat16 or wider, within the bound.
A program may use at most 64 MiB of HBM per device.

v0:
```python
import math
import jax
import jax.numpy as jnp
from jax import lax
from jax.sharding import PartitionSpec as P

EPS = 1e-06
RIDGE = 1.0


def design(epochs, count):
    index = jnp.arange(count, dtype=jnp.int32)
    days = index.astype(jnp.float32)
    scaled = 2.0 * days / (count - 1) - 1.0
    years = days * 12.0 / 365.25
    smooth = jnp.stack(
        [
            jnp.ones_like(days),
            scaled,
            scaled * scaled,
            scaled * scaled * scaled,
            jnp.sin(2.0 * math.pi * years),
            jnp.cos(2.0 * math.pi * years),
            jnp.sin(4.0 * math.pi * years),
            jnp.cos(4.0 * math.pi * years),
        ],
        axis=1,
    )
    jumps = (index[:, None] >= epochs[None, :]).astype(jnp.float32)
    return jnp.concatenate([smooth, jumps], axis=1)


def fit_operator(epochs, count):
    matrix = design(epochs, count)
    normal = jnp.dot(
        matrix.T, matrix, precision=lax.Precision.HIGHEST, preferred_element_type=jnp.float32
    )
    normal = normal + RIDGE * jnp.eye(matrix.shape[1], dtype=jnp.float32)
    factor = jnp.linalg.cholesky(normal)
    return jax.scipy.linalg.cho_solve((factor, True), matrix.T)


def incidence_matrix(pairs, count):
    dates = jnp.arange(count, dtype=jnp.int32)
    later = (pairs[:, 1:2] == dates[None, :]).astype(jnp.float32)
    earlier = (pairs[:, 0:1] == dates[None, :]).astype(jnp.float32)
    return later - earlier


def shards(ifgs, pairs, pseudo_inverse, ref_pixels, epochs):
    row_count = ifgs.shape[1]
    col_total = ifgs.shape[2]
    col_count = col_total // lax.axis_size("ifg")
    region_size = ref_pixels.shape[0]
    date_count = pseudo_inverse.shape[0]
    tile_index = lax.axis_index("tile")
    ifg_index = lax.axis_index("ifg")
    ref_row = ref_pixels // col_total
    ref_col = ref_pixels % col_total
    row_rel = ref_row - tile_index * row_count
    in_tile = (row_rel >= 0) & (row_rel < row_count)
    row_safe = jnp.clip(row_rel, 0, row_count - 1)
    regrouped = lax.all_to_all(ifgs, "ifg", split_axis=2, concat_axis=0, tiled=True)
    col_rel = ref_col - ifg_index * col_count
    in_block = in_tile & (col_rel >= 0) & (col_rel < col_count)
    col_safe = jnp.clip(col_rel, 0, col_count - 1)
    values = regrouped[:, row_safe, col_safe].astype(jnp.float32)
    partial_value = jnp.sum(jnp.where(in_block[None, :], values, 0.0), axis=1)
    totals = lax.psum(partial_value, ("ifg", "tile"))
    corrected = (regrouped.astype(jnp.float32) - (totals / region_size)[:, None, None]).astype(
        jnp.bfloat16
    )
    pixel_rows = corrected.reshape(corrected.shape[0], row_count * col_count)
    displacement = jnp.dot(
        lax.all_gather(pseudo_inverse, "ifg", axis=1, tiled=True),
        pixel_rows,
        preferred_element_type=jnp.float32,
    )
    operator = fit_operator(epochs, date_count)
    coeffs = jnp.dot(
        operator, displacement, precision=lax.Precision.HIGHEST, preferred_element_type=jnp.float32
    )
    incidence = incidence_matrix(pairs, date_count)
    predicted = jnp.dot(
        incidence, displacement, precision=lax.Precision.HIGHEST, preferred_element_type=jnp.float32
    )
    misfit = pixel_rows.astype(jnp.float32) - predicted
    spread = jnp.sqrt(jnp.mean(misfit * misfit, axis=0) + EPS)
    return (
        coeffs.reshape(operator.shape[0], row_count, col_count),
        spread.reshape(row_count, col_count),
    )


def solution(mesh):
    in_specs = (P("ifg", "tile", None), P(), P(None, "ifg"), P(), P())
    out_specs = (P(None, "tile", "ifg"), P("tile", "ifg"))
    return jax.shard_map(shards, mesh=mesh, in_specs=in_specs, out_specs=out_specs, check_vma=False)
```

profile of v0, /device:TPU:1, one launch (start us, length us, event | category | flops | bytes accessed | tf_op | source)
XLA Modules:
  0.0 324.9 jit_solution(13141437848219759013)
XLA Ops:
  0.6 15.8 %copy.18 = bf16[9,2,16384]{0,1,2:T(2,128)(2,1)} copy(bf16[9,2,16384]{2,1,0:T(2,128)(2,1)} %param.5) | data formatting | bytes 1179648 | tf_op args[0]
  16.4 18.2 %reshape.101 = bf16[128,2,1152]{2,1,0:T(2,128)(2,1)} reshape(bf16[16384,2,9]{2,1,0:T(2,128)(2,1)} %bitcast.43) | data formatting | bytes 1179648
  34.7 20.5 %all-to-all-start = ((bf16[128,2,1152]{2,1,0:T(2,128)(2,1)}), bf16[128,2,1152]{2,1,0:T(2,128)(2,1)S(1)}, u32[]{:S(2)}, u32[]{:S(2)}) async-start(bf16[128,2,1152]{2,1,0:T(2,128)(2,1)} %reshape.101), calls=%async_computation | async-start | bytes 1179648 | tf_op jit(solution)/shard_map/all_to_all | solution.py:63
  55.2 0.1 fusion.19
  55.3 0.1 fusion.21
  55.4 0.1 multiply_add_fusion
  55.5 0.0 copy-done.2
  55.5 0.1 fusion.10
  55.6 0.2 fusion.35
  55.7 0.1 copy.17
  55.8 1.5 cholesky.17
  57.3 0.6 compare_reduce_fusion
  57.9 0.6 fusion.11
  58.6 1.2 custom-call.10
  59.8 118.4 %all-gather = bf16[128,9,300]{2,1,0:T(8,128)(2,1)S(1)} all-gather(bf16[1,9,300]{2,1,0:T(8,128)(2,1)S(1)} %bitcast.47), channel_id=1, replica_groups=mesh['ifg'=128,'tile'=4] {'ifg'}, dimensions={0}, use_global_device_ids=true | all-gather | bytes 696600 | tf_op jit(solution)/shard_map/all_gather | solution.py:75
  178.2 0.7 reshape.98
  178.9 0.0 copy-done.1
  179.0 0.2 fusion.14
  179.2 0.2 fusion.12
  179.4 0.0 all-to-all-done
  179.4 19.3 %reshape.102 = bf16[16384,2,9]{2,1,0:T(2,128)(2,1)} reshape(bf16[128,2,1152]{2,1,0:T(2,128)(2,1)S(1)} %all-to-all-done) | data formatting | bytes 1179648
  198.7 16.6 %copy.19 = bf16[9,2,128,128]{3,1,0,2:T(2,128)(2,1)S(1)} copy(bf16[9,2,128,128]{0,1,3,2:T(2,128)(2,1)} %bitcast.42) | data formatting | bytes 1179648 | tf_op jit(solution)/shard_map/all_to_all | solution.py:63
  215.2 0.4 bitcast_convert_fusion
  215.7 0.6 copy.20
  216.3 1.2 gather_fusion
  217.5 0.1 select_reduce_fusion
  217.6 102.6 %psum.7 = f32[1152]{0:T(1024)S(1)} all-reduce(f32[1152]{0:T(1024)S(1)} %select_reduce_fusion), channel_id=1, replica_groups=mesh['ifg'=128,'tile'=4] {'ifg','tile'}, use_global_device_ids=true, to_apply=%region_3.4 | all-reduce | flops 1152 | bytes 9216 | tf_op jit(solution)/shard_map/psum | solution.py:69
  320.1 0.7 fusion.31
  320.8 0.2 fusion.36
  321.0 0.7 reshape.77
  321.7 2.6 fusion.4
  324.4 0.6 sqrt_bitcast_fusion
  (15 shorter events, 0.2 us)
Async XLA Ops:
  34.7 20.8 %copy-start.2 = (s32[8]{0:T(128)S(1)}, s32[8]{0:T(128)}, u32[]{:S(2)}) copy-start(s32[8]{0:T(128)} %param.9) | copy-start | bytes 100
  34.7 25.2 %copy-start = (bf16[300,9]{0,1:T(8,128)(2,1)S(1)}, bf16[300,9]{0,1:T(8,128)(2,1)}, u32[]{:S(2)}) copy-start(bf16[300,9]{0,1:T(8,128)(2,1)} %param.7) | copy-start | bytes 16204
  34.7 144.7 %all-to-all-start = ((bf16[128,2,1152]{2,1,0:T(2,128)(2,1)}), bf16[128,2,1152]{2,1,0:T(2,128)(2,1)S(1)}, u32[]{:S(2)}, u32[]{:S(2)}) async-start(bf16[128,2,1152]{2,1,0:T(2,128)(2,1)} %reshape.101), calls=%async_computation | async-start | bytes 1179648 | tf_op jit(solution)/shard_map/all_to_all | solution.py:63
  178.2 0.7 copy-start.1
  178.2 0.7 copy-start.3
where the time goes:
time: 327 us; the launch traced here: 325 us
  blocking collectives  221 us (68%)
  local copies, waits for them, and re-layouts  73.1 us (22%)
  starting transfers between devices  20.5 us (6%)
  other arithmetic  5.45 us (2%)
  matrix products  4.07 us (1%)
    all_gather x1, blocking collectives, shards(): lax.all_gather(pseudo_inverse, 'ifg', axis=1, tiled=True)  118 us
    psum x1, blocking collectives, shards(): totals = lax.psum(partial_value, ('ifg', 'tile'))  103 us
    unnamed x12, local copies, waits for them, and re-layouts  54 us
    all_to_all x1, starting transfers between devices, shards(): lax.all_to_all(ifgs, 'ifg', split_axis=2, concat_axis=0, tiled=True)  20.5 us
    all_to_all x2, local copies, waits for them, and re-layouts, shards(): lax.all_to_all(ifgs, 'ifg', split_axis=2, concat_axis=0, tiled=True)  17.2 us
  transfers between devices with their start and end apart: 1, of which 0 were waited for; matrix products, arithmetic and copies ran while one was open for 2% of the time, Pallas kernels for 0%

commit v1 on v0

--- a/solution.py
+++ b/solution.py
@@ -6,6 +6,11 @@
 
 EPS = 1e-06
 RIDGE = 1.0
+
+
+def exchange_gather(x, name, dim):
+    sent = jnp.stack([x] * lax.axis_size(name))
+    return jnp.concatenate(lax.all_to_all(sent, name, 0, 0), axis=dim)
 
 
 def design(epochs, count):
@@ -72,9 +77,7 @@
     )
     pixel_rows = corrected.reshape(corrected.shape[0], row_count * col_count)
     displacement = jnp.dot(
-        lax.all_gather(pseudo_inverse, "ifg", axis=1, tiled=True),
-        pixel_rows,
-        preferred_element_type=jnp.float32,
+        exchange_gather(pseudo_inverse, "ifg", 1), pixel_rows, preferred_element_type=jnp.float32
     )
     operator = fit_operator(epochs, date_count)
     coeffs = jnp.dot(

time: 327 us -> 261 us (0.80)
  blocking collectives: 221 us -> 106 us
  waiting for transfers between devices: 0.01 us -> 32.5 us
  starting transfers between devices: 20.5 us -> 27.9 us
  local copies, waits for them, and re-layouts: 73.1 us -> 78.5 us
  other arithmetic: 5.45 us -> 8.85 us
    all_gather x1 -> x0, blocking collectives: 118 us -> none  [shards(): lax.all_gather(pseudo_inverse, 'ifg', axis=1, tiled=True)]
    all_to_all x1, waiting for transfers between devices: 0.01 us -> 32.5 us  [shards(): lax.all_to_all(ifgs, 'ifg', split_axis=2, concat_axis=0, tiled=True)]
    all_to_all x0 -> x1, starting transfers between devices: none -> 7.55 us  [exchange_gather(): return jnp.concatenate(lax.all_to_all(sent, name, 0, 0), axis=dim)]
    unnamed x12 -> x18, local copies, waits for them, and re-layouts: 54 us -> 58.3 us
    psum x1, blocking collectives: 103 us -> 106 us  [shards(): totals = lax.psum(partial_value, ('ifg', 'tile'))]
  transfers between devices with their start and end apart: 1 -> 2, of which waited for: 0 -> 1; matrix products, arithmetic and copies ran while one was open for 2% -> 19% of each run, Pallas kernels for 0% -> 0%
where the time goes in v1:
time: 261 us; the launch traced here: 259 us
  blocking collectives  106 us (41%)
  local copies, waits for them, and re-layouts  78.5 us (30%)
  waiting for transfers between devices  32.5 us (12%)
  starting transfers between devices  27.9 us (11%)
  other arithmetic  8.85 us (3%)
  matrix products  3.87 us (1%)
    psum x1, blocking collectives, shards(): totals = lax.psum(partial_value, ('ifg', 'tile'))  106 us
    unnamed x18, local copies, waits for them, and re-layouts  58.3 us
    all_to_all x1, waiting for transfers between devices, shards(): lax.all_to_all(ifgs, 'ifg', split_axis=2, concat_axis=0, tiled=True)  32.5 us
    all_to_all x1, starting transfers between devices, shards(): lax.all_to_all(ifgs, 'ifg', split_axis=2, concat_axis=0, tiled=True)  20.4 us
    all_to_all x2, local copies, waits for them, and re-layouts, shards(): lax.all_to_all(ifgs, 'ifg', split_axis=2, concat_axis=0, tiled=True)  17.2 us
    all_to_all x1, starting transfers between devices, exchange_gather(): return jnp.concatenate(lax.all_to_all(sent, name, 0, 0), axis=dim)  7.55 us
  transfers between devices with their start and end apart: 2, of which 1 were waited for; matrix products, arithmetic and copies ran while one was open for 19% of the time, Pallas kernels for 0%

profile of v1, /device:TPU:1, one launch (start us, length us, event | category | flops | bytes accessed | tf_op | source)
XLA Modules:
  0.0 258.8 jit_solution(2375770332111473166)
XLA Ops:
  0.6 15.8 %copy.19 = bf16[9,2,16384]{0,1,2:T(2,128)(2,1)} copy(bf16[9,2,16384]{2,1,0:T(2,128)(2,1)} %param.5) | data formatting | bytes 1179648 | tf_op args[0]
  16.4 18.2 %reshape.117 = bf16[128,2,1152]{2,1,0:T(2,128)(2,1)} reshape(bf16[16384,2,9]{2,1,0:T(2,128)(2,1)} %bitcast.54) | data formatting | bytes 1179648
  34.7 20.4 %all-to-all-start = ((bf16[128,2,1152]{2,1,0:T(2,128)(2,1)}), bf16[128,2,1152]{2,1,0:T(2,128)(2,1)S(1)}, u32[]{:S(2)}, u32[]{:S(2)}) async-start(bf16[128,2,1152]{2,1,0:T(2,128)(2,1)} %reshape.117), calls=%async_computation | async-start | bytes 1179648 | tf_op jit(solution)/shard_map/all_to_all | solution.py:68
  55.1 0.1 broadcast_bitcast_fusion
  55.3 2.6 reshape.115
  58.2 32.5 %all-to-all-done = bf16[128,2,1152]{2,1,0:T(2,128)(2,1)S(1)} async-done(((bf16[128,2,1152]{2,1,0:T(2,128)(2,1)}), bf16[128,2,1152]{2,1,0:T(2,128)(2,1)S(1)}, u32[]{:S(2)}, u32[]{:S(2)}) %all-to-all-start) | async-done | bytes 589856 | tf_op jit(solution)/shard_map/all_to_all | solution.py:68
  90.7 7.6 %all-to-all-start.1 = ((bf16[128,2,1350]{2,1,0:T(2,128)(2,1)}), bf16[128,2,1350]{2,1,0:T(2,128)(2,1)S(1)}, u32[]{:S(2)}, u32[]{:S(2)}) async-start(bf16[128,2,1350]{2,1,0:T(2,128)(2,1)} %reshape.115), calls=%async_computation.1 | async-start | bytes 1441792 | tf_op jit(solution)/shard_map/all_to_all | solution.py:13
  98.3 0.1 fusion.36
  98.5 1.5 cholesky.17
  100.0 0.6 compare_reduce_fusion
  100.6 0.6 fusion.14
  101.3 1.2 custom-call.10
  102.6 0.2 fusion.17
  102.9 0.2 fusion.15
  103.0 19.3 %reshape.118 = bf16[16384,2,9]{2,1,0:T(2,128)(2,1)} reshape(bf16[128,2,1152]{2,1,0:T(2,128)(2,1)S(1)} %all-to-all-done) | data formatting | bytes 1179648
  122.3 16.6 %copy.20 = bf16[9,2,128,128]{3,1,0,2:T(2,128)(2,1)S(1)} copy(bf16[9,2,128,128]{0,1,3,2:T(2,128)(2,1)} %bitcast.53) | data formatting | bytes 1179648 | tf_op jit(solution)/shard_map/all_to_all | solution.py:68
  138.9 0.6 copy.21
  139.5 1.2 gather_fusion
  140.7 0.1 select_reduce_fusion
  140.8 106.2 %psum.7 = f32[1152]{0:T(1024)S(1)} all-reduce(f32[1152]{0:T(1024)S(1)} %select_reduce_fusion), channel_id=1, replica_groups=mesh['ifg'=128,'tile'=4] {'ifg','tile'}, use_global_device_ids=true, to_apply=%region_3.4 | all-reduce | flops 1152 | bytes 9216 | tf_op jit(solution)/shard_map/psum | solution.py:74
  247.0 0.2 sub.54
  247.2 2.4 subtract_convert_fusion
  249.6 1.4 bitcast_convert_fusion
  251.0 1.9 reshape.116
  253.0 0.2 bitcast_bitcast_fusion
  253.1 0.7 reshape.92
  253.8 0.4 copy-done.1
  254.2 0.5 fusion.10
  254.7 0.2 fusion.37
  254.9 0.7 reshape.93
  255.5 2.7 %fusion.4 = f32[256]{0:T(256)S(1)} fusion(f32[256,300]{0,1:T(8,128)S(1)} %fusion.10, s32[1152]{0:T(1024)S(1)} %get-tuple-element.3, s32[1152]{0:T(1024)S(1)} %get-tuple-element.2, f32[144,8,2,128]{3,2,1,0:T(2,128)S(1)} %bitcast.57, f32[1152]{0:T(1024)S(1)} %broadcast_multiply_fusion), kind=kOutput, calls=%fused_computation.8 | convolution fusion | flops 1065180416 | bytes 1501696 | tf_op jit(solution)/shard_map/dot_general | solution.py:87
  258.2 0.6 sqrt_bitcast_fusion
  (26 shorter events, 0.6 us)
Async XLA Ops:
  0.6 54.4 %copy-start = (bf16[300,9]{0,1:T(8,128)(2,1)S(1)}, bf16[300,9]{0,1:T(8,128)(2,1)}, u32[]{:S(2)}) copy-start(bf16[300,9]{0,1:T(8,128)(2,1)} %param.7) | copy-start | bytes 16204
  34.7 56.0 %all-to-all-start = ((bf16[128,2,1152]{2,1,0:T(2,128)(2,1)}), bf16[128,2,1152]{2,1,0:T(2,128)(2,1)S(1)}, u32[]{:S(2)}, u32[]{:S(2)}) async-start(bf16[128,2,1152]{2,1,0:T(2,128)(2,1)} %reshape.117), calls=%async_computation | async-start | bytes 1179648 | tf_op jit(solution)/shard_map/all_to_all | solution.py:68
  55.1 3.0 %copy-start.4 = (s32[8]{0:T(128)S(1)}, s32[8]{0:T(128)}, u32[]{:S(2)}) copy-start(s32[8]{0:T(128)} %param.9) | copy-start | bytes 100
  55.2 47.3 %copy-start.3 = (s32[1152,2]{0,1:T(2,128)S(1)}, s32[1152,2]{0,1:T(2,128)}, u32[]{:S(2)}) copy-start(s32[1152,2]{0,1:T(2,128)} %param.6) | copy-start | bytes 27652
  55.2 47.3 %copy-start.5 = (s32[64]{0:T(128)S(1)}, s32[64]{0:T(128)}, u32[]{:S(2)}) copy-start(s32[64]{0:T(128)} %param.8) | copy-start | bytes 772
  90.7 160.3 %all-to-all-start.1 = ((bf16[128,2,1350]{2,1,0:T(2,128)(2,1)}), bf16[128,2,1350]{2,1,0:T(2,128)(2,1)S(1)}, u32[]{:S(2)}, u32[]{:S(2)}) async-start(bf16[128,2,1350]{2,1,0:T(2,128)(2,1)} %reshape.115), calls=%async_computation.1 | async-start | bytes 1441792 | tf_op jit(solution)/shard_map/all_to_all | solution.py:13
  253.1 1.1 copy-start.1
  253.8 1.7 copy-start.2

commit v2 on v0

--- a/solution.py
+++ b/solution.py
@@ -66,7 +66,8 @@
     col_safe = jnp.clip(col_rel, 0, col_count - 1)
     values = regrouped[:, row_safe, col_safe].astype(jnp.float32)
     partial_value = jnp.sum(jnp.where(in_block[None, :], values, 0.0), axis=1)
-    totals = lax.psum(partial_value, ("ifg", "tile"))
+    half = lax.psum(partial_value, "tile")
+    totals = lax.psum(half, "ifg")
     corrected = (regrouped.astype(jnp.float32) - (totals / region_size)[:, None, None]).astype(
         jnp.bfloat16
     )

time: 327 us -> 486 us (1.49)
  blocking collectives: 221 us -> 380 us
    psum x1 -> x2, blocking collectives: 103 us -> 261 us  [the longest x1 252 us: shards(): totals = lax.psum(half, 'ifg')]
  transfers between devices with their start and end apart: 1 -> 1, of which waited for: 0 -> 0; matrix products, arithmetic and copies ran while one was open for 2% -> 1% of each run, Pallas kernels for 0% -> 0%
where the time goes in v2:
time: 486 us; the launch traced here: 484 us
  blocking collectives  380 us (78%)
  local copies, waits for them, and re-layouts  73.1 us (15%)
  starting transfers between devices  20.5 us (4%)
  other arithmetic  5.45 us (1%)
    psum x1, blocking collectives, shards(): totals = lax.psum(half, 'ifg')  252 us
    all_gather x1, blocking collectives, shards(): lax.all_gather(pseudo_inverse, 'ifg', axis=1, tiled=True)  118 us
    unnamed x12, local copies, waits for them, and re-layouts  54 us
    all_to_all x1, starting transfers between devices, shards(): lax.all_to_all(ifgs, 'ifg', split_axis=2, concat_axis=0, tiled=True)  20.5 us
    all_to_all x2, local copies, waits for them, and re-layouts, shards(): lax.all_to_all(ifgs, 'ifg', split_axis=2, concat_axis=0, tiled=True)  17.2 us
  transfers between devices with their start and end apart: 1, of which 0 were waited for; matrix products, arithmetic and copies ran while one was open for 1% of the time, Pallas kernels for 0%

profile of v2, /device:TPU:1, one launch (start us, length us, event | category | flops | bytes accessed | tf_op | source)
XLA Modules:
  0.0 483.6 jit_solution(12632343201989399949)
XLA Ops:
  0.6 15.8 %copy.18 = bf16[9,2,16384]{0,1,2:T(2,128)(2,1)} copy(bf16[9,2,16384]{2,1,0:T(2,128)(2,1)} %param.5) | data formatting | bytes 1179648 | tf_op args[0]
  16.4 18.2 %reshape.101 = bf16[128,2,1152]{2,1,0:T(2,128)(2,1)} reshape(bf16[16384,2,9]{2,1,0:T(2,128)(2,1)} %bitcast.43) | data formatting | bytes 1179648
  34.7 20.5 %all-to-all-start = ((bf16[128,2,1152]{2,1,0:T(2,128)(2,1)}), bf16[128,2,1152]{2,1,0:T(2,128)(2,1)S(1)}, u32[]{:S(2)}, u32[]{:S(2)}) async-start(bf16[128,2,1152]{2,1,0:T(2,128)(2,1)} %reshape.101), calls=%async_computation | async-start | bytes 1179648 | tf_op jit(solution)/shard_map/all_to_all | solution.py:63
  55.2 0.1 fusion.19
  55.3 0.1 fusion.21
  55.4 0.1 multiply_add_fusion
  55.5 0.1 fusion.10
  55.6 0.2 fusion.35
  55.7 0.1 copy.17
  55.8 1.5 cholesky.17
  57.3 0.6 compare_reduce_fusion
  57.9 0.6 fusion.11
  58.6 1.2 custom-call.10
  59.8 118.4 %all-gather = bf16[128,9,300]{2,1,0:T(8,128)(2,1)S(1)} all-gather(bf16[1,9,300]{2,1,0:T(8,128)(2,1)S(1)} %bitcast.47), channel_id=1, replica_groups=mesh['ifg'=128,'tile'=4] {'ifg'}, dimensions={0}, use_global_device_ids=true | all-gather | bytes 696600 | tf_op jit(solution)/shard_map/all_gather | solution.py:76
  178.2 0.7 reshape.98
  178.9 0.0 copy-done.1
  179.0 0.2 fusion.14
  179.2 0.2 fusion.12
  179.4 0.0 all-to-all-done
  179.4 19.3 %reshape.102 = bf16[16384,2,9]{2,1,0:T(2,128)(2,1)} reshape(bf16[128,2,1152]{2,1,0:T(2,128)(2,1)S(1)} %all-to-all-done) | data formatting | bytes 1179648
  198.7 16.6 %copy.19 = bf16[9,2,128,128]{3,1,0,2:T(2,128)(2,1)S(1)} copy(bf16[9,2,128,128]{0,1,3,2:T(2,128)(2,1)} %bitcast.42) | data formatting | bytes 1179648 | tf_op jit(solution)/shard_map/all_to_all | solution.py:63
  215.2 0.4 bitcast_convert_fusion
  215.7 0.6 copy.20
  216.3 1.2 gather_fusion
  217.5 0.1 select_reduce_fusion
  217.6 8.8 %psum.14 = f32[1152]{0:T(1024)S(1)} all-reduce(f32[1152]{0:T(1024)S(1)} %select_reduce_fusion), channel_id=1, replica_groups=mesh['ifg'=128,'tile'=4] {'tile'}, use_global_device_ids=true, to_apply=%region_3.4 | all-reduce | flops 1152 | bytes 9216 | tf_op jit(solution)/shard_map/psum | solution.py:69
  226.4 252.4 %psum.15 = f32[1152]{0:T(1024)S(1)} all-reduce(f32[1152]{0:T(1024)S(1)} %psum.14), channel_id=1, replica_groups=mesh['ifg'=128,'tile'=4] {'ifg'}, use_global_device_ids=true, to_apply=%region_4.5 | all-reduce | flops 1152 | bytes 9216 | tf_op jit(solution)/shard_map/psum | solution.py:70
  478.8 0.7 fusion.31
  479.5 0.2 fusion.36
  479.7 0.7 reshape.77
  480.4 2.6 fusion.4
  483.1 0.6 sqrt_bitcast_fusion
  (16 shorter events, 0.2 us)
Async XLA Ops:
  34.7 20.8 %copy-start.2 = (s32[8]{0:T(128)S(1)}, s32[8]{0:T(128)}, u32[]{:S(2)}) copy-start(s32[8]{0:T(128)} %param.9) | copy-start | bytes 100
  34.7 25.2 %copy-start = (bf16[300,9]{0,1:T(8,128)(2,1)S(1)}, bf16[300,9]{0,1:T(8,128)(2,1)}, u32[]{:S(2)}) copy-start(bf16[300,9]{0,1:T(8,128)(2,1)} %param.7) | copy-start | bytes 16204
  34.7 144.7 %all-to-all-start = ((bf16[128,2,1152]{2,1,0:T(2,128)(2,1)}), bf16[128,2,1152]{2,1,0:T(2,128)(2,1)S(1)}, u32[]{:S(2)}, u32[]{:S(2)}) async-start(bf16[128,2,1152]{2,1,0:T(2,128)(2,1)} %reshape.101), calls=%async_computation | async-start | bytes 1179648 | tf_op jit(solution)/shard_map/all_to_all | solution.py:63
  178.2 0.7 copy-start.1
  178.2 0.7 copy-start.3
